TPU v7x, 256 devices: a whole 4x4x8 slice. The times are simulated.
256 devices in a mesh: row: 4 (over y_hi, core), col: 8 (over z), seq: 8 (over x, y_lo).
Axes of the slice: x: 4, y: 4 (y_hi: 2, y_lo: 2; y = y_hi * 2 + y_lo), z: 8, core: 2. Of those that a mesh axis runs over, the one named last changes fastest.
Arguments:
- queries: bfloat16 [4, 2048, 8192], P('row', 'seq', 'col'), may hold values from -120 to 120
- rotated_key_heads: bfloat16 [4, 2048, 1024], P('row', 'seq', 'col'), may hold values from -7 to 7
- value_head_states: bfloat16 [4, 2048, 1024], P('row', 'seq', 'col'), may hold values from -6 to 6
- document_index: int32 [4, 2048], P('row'), may hold values from 0 to 3, never falling along the last dimension, each value on 1 to 1024 neighbouring positions
- output_projection_weight: bfloat16 [8192, 8192], P('col', 'row'), may hold values from -0.1875 to 0.1875
- frozen_down_factor: bfloat16 [8192, 256], P('col'), may hold values from -0.1875 to 0.1875
- trained_up_factor: bfloat16 [256, 8192], P(None, 'row'), may hold values from -0.125 to 0.125
- correction_tiles: bfloat16 [4, 8, 2, 128, 128], P('row', 'col'), may hold values from -1.1953125 to 1.1953125
- tile_placement: int32 [4, 8, 2, 2], P('row', 'col'), may hold values from 0 to 15, as said below
- cotangent: bfloat16 [4, 2048, 8192], P(None, 'seq', ('row', 'col')), may hold values from -0.06591797 to 0.06591797
Outputs:
- projected: bfloat16 [4, 2048, 8192], P(None, 'seq', ('row', 'col'))
- up_factor_gradient: float32 [256, 8192], P(None, 'row')
- grad_tiles: float32 [4, 8, 2, 128, 128], P('row', 'col')
Inputs may be any that keep to these rules, and one draw needn't show every extreme that they name: `tile_placement`: inside one block of the weight grid the 2 tiles are different; entry 0 is a tile row below 8, entry 1 a tile column below 16.
All inputs are finite; a program needn't handle non-finite values.
Results may differ from a plain program's by a relative error of at most 0.0054.
Values may be sent and summed in bfloat16 or wider, within the bound.
A program may use at most 128 MiB of HBM per device.

v0:
```python
import jax
import jax.numpy as jnp
from jax import lax
from jax.sharding import PartitionSpec as P

QUERY_HEADS = 64
KEY_VALUE_HEADS = 8
HEAD_WIDTH = 128
TILE = 128


low_rank_factor = 2.0


def sent_together(arrays, axis, dim, along):
    ends, at = ([], 0)
    for a in arrays[:-1]:
        at += a.shape[along]
        ends.append(at)
    both = jnp.concatenate(arrays, axis=along)
    return tuple(jnp.split(lax.all_gather(both, axis, axis=dim, tiled=True), ends, axis=along))


def in_order(pieces, dim):
    shape = list(pieces.shape[1:])
    shape[dim] *= pieces.shape[0]
    return jnp.moveaxis(pieces, 0, dim).reshape(shape)


def sent_to_all(shard, axis):
    peers = lax.axis_size(axis)
    return lax.all_to_all(
        jnp.broadcast_to(shard[None], (peers, *shard.shape)), axis, 0, 0, tiled=True
    )


def collect(shard, axis, dim):
    return in_order(sent_to_all(shard, axis), dim)


def taken_together(shard, axis):
    return sent_to_all(shard, axis).sum(axis=0)


def in_one(arrays, axis):
    ends = [0]
    for a in arrays:
        ends.append(ends[-1] + a.size)
    running = taken_together(jnp.concatenate([a.ravel() for a in arrays]), axis)
    return tuple((running[b:e].reshape(a.shape) for a, b, e in zip(arrays, ends, ends[1:])))


def attend(queries, key_rows, values, documents, query_start):
    item_count, query_len, shared_heads, query_group_width, head_size = queries.shape
    key_len = key_rows.shape[1]
    block_rows = min(512, query_len)
    block_count = query_len // block_rows
    score_scale = head_size ** (-0.5)
    key_pos = jnp.arange(key_len, dtype=jnp.int32)

    def one_block(block_index):
        row_start = block_index * block_rows
        scores = (
            jnp.einsum("nqkgd,nskd->nkgqs", queries, key_rows, preferred_element_type=jnp.float32)
            * score_scale
        )
        query_pos = query_start + row_start + jnp.arange(block_rows, dtype=jnp.int32)
        query_docs = lax.dynamic_slice_in_dim(documents, query_start + row_start, block_rows, 1)
        visible = (key_pos[None, None, :] <= query_pos[None, :, None]) & (
            documents[:, None, :] == query_docs[:, :, None]
        )
        visible = visible[:, None, None, :, :]
        row_max = jnp.max(jnp.where(visible, scores, -jnp.inf), axis=-1, keepdims=True)
        weights = jnp.exp(jnp.where(visible, scores - row_max, -jnp.inf))
        row_total = jnp.sum(weights, axis=-1)
        mixed_rows = jnp.einsum(
            "nkgqs,nskd->nqkgd",
            weights.astype(jnp.bfloat16),
            values,
            preferred_element_type=jnp.float32,
        )
        mixed_rows = mixed_rows / jnp.moveaxis(row_total, 3, 1)[..., None]
        return mixed_rows.astype(jnp.bfloat16)

    results = lax.map(one_block, jnp.arange(block_count, dtype=jnp.int32))
    return jnp.moveaxis(results, 0, 1).reshape(
        item_count, query_len, shared_heads * query_group_width * head_size
    )


def local(
    queries,
    rotated_key_heads,
    value_head_states,
    document_index,
    output_projection_weight,
    frozen_down_factor,
    trained_up_factor,
    correction_tiles,
    tile_placement,
    cotangent,
):
    leading = queries.shape[0]
    local_len = queries.shape[1]
    col_width = queries.shape[2]
    shared_col = rotated_key_heads.shape[2] // HEAD_WIDTH
    query_group_width = QUERY_HEADS // KEY_VALUE_HEADS
    key_full, value_full = sent_together((rotated_key_heads, value_head_states), "seq", 1, 0)
    full_len = key_full.shape[1]
    shaped = queries.reshape(leading, local_len, shared_col, query_group_width, HEAD_WIDTH)
    attention_output = attend(
        shaped,
        key_full.reshape(leading, full_len, shared_col, HEAD_WIDTH),
        value_full.reshape(leading, full_len, shared_col, HEAD_WIDTH),
        document_index,
        lax.axis_index("seq") * local_len,
    )
    gathered = collect(attention_output, "row", 0)
    sequence_rows = gathered.shape[0]
    seq_total = sequence_rows * local_len
    flattened_rows = gathered.reshape(seq_total, col_width)
    out_width = output_projection_weight.shape[1]
    in_tiles = col_width // TILE
    out_tiles = out_width // TILE
    coords = tile_placement.reshape(-1, 2)
    tile_in = coords[:, 0]
    tile_out = coords[:, 1]
    tile_values = correction_tiles.reshape(-1, TILE, TILE)
    partial_value = jnp.dot(
        flattened_rows, output_projection_weight, preferred_element_type=jnp.float32
    )
    low_rank_piece = jnp.dot(flattened_rows, frozen_down_factor, preferred_element_type=jnp.float32)
    picked = flattened_rows.reshape(seq_total, in_tiles, TILE)[:, tile_in]
    tile_terms = jnp.einsum("tbi,bio->tbo", picked, tile_values, preferred_element_type=jnp.float32)
    partial_value = (
        partial_value.reshape(seq_total, out_tiles, TILE)
        .at[:, tile_out]
        .add(tile_terms)
        .reshape(seq_total, out_width)
    )
    combined_output = lax.psum_scatter(
        partial_value.reshape(sequence_rows, local_len, out_width),
        "col",
        scatter_dimension=2,
        tiled=True,
    )
    low_rank_inner = lax.psum(low_rank_piece, "col").astype(jnp.bfloat16)
    segment_width = combined_output.shape[2]
    up_factor_piece = lax.dynamic_slice_in_dim(
        trained_up_factor, lax.axis_index("col") * segment_width, segment_width, 1
    )
    combined_output = combined_output + low_rank_factor * jnp.dot(
        low_rank_inner, up_factor_piece, preferred_element_type=jnp.float32
    ).reshape(combined_output.shape)
    cot_full = lax.all_gather(cotangent, "col", axis=2, tiled=True)
    cot_flat = cot_full.reshape(seq_total, out_width)
    cot_picked = cot_flat.reshape(seq_total, out_tiles, TILE)[:, tile_out]
    tile_grad = jnp.einsum("tbi,tbo->bio", picked, cot_picked, preferred_element_type=jnp.float32)
    cot_own = cotangent.reshape(seq_total, cotangent.shape[2])
    up_slice = low_rank_factor * lax.dot_general(
        low_rank_inner, cot_own, (((0,), (0,)), ((), ())), preferred_element_type=jnp.float32
    )
    slice_sum, tile_total = in_one((up_slice, tile_grad), "seq")
    up_factor_gradient = collect(slice_sum, "col", 1)
    return (
        combined_output.astype(jnp.bfloat16),
        up_factor_gradient,
        tile_total.reshape(correction_tiles.shape),
    )


def solution(mesh):
    placed = (
        P("row", "seq", "col"),
        P("row", "seq", "col"),
        P("row", "seq", "col"),
        P("row", None),
        P("col", "row"),
        P("col", None),
        P(None, "row"),
        P("row", "col", None, None, None),
        P("row", "col", None, None),
        P(None, "seq", ("row", "col")),
    )
    return jax.shard_map(
        local,
        mesh=mesh,
        in_specs=placed,
        out_specs=(
            P(None, "seq", ("row", "col")),
            P(None, "row"),
            P("row", "col", None, None, None),
        ),
        check_vma=False,
    )
```

profile of v0, /device:TPU:6, one launch (start us, length us, event | category | flops | bytes accessed | tf_op | source)
XLA Modules:
  0.0 349.9 jit_solution(7018468490969759056)
XLA Ops:
  12.8 40.4 %all-gather.3.cloned.1.call-done = bf16[2,2048,128]{2,1,0:T(8,128)(2,1)} async-done(((bf16[2,256,128]{2,1,0:T(8,128)(2,1)}), bf16[2,2048,128]{2,1,0:T(8,128)(2,1)}) %all-gather.3.cloned.1.call-update) | async-done | bytes 1048592 | tf_op jit(solution)/shard_map/all_gather | solution.py:21
  53.1 8.2 %fusion = (f32[8,256]{1,0:T(8,128)S(1)}, f32[2048,256,8]{1,0,2:T(8,128)}) fusion(pred[256,2048]{0,1:T(8,128)(4,1)S(1)} %fusion.9, bf16[256,8,128]{2,1,0:T(8,128)(2,1)S(1)} %bitcast.111, bf16[2,2048,128]{2,1,0:T(8,128)(2,1)} %all-gather.3.cloned.1.call-done), kind=kOutput, calls=%fused_computation.5 | convolution fusion | flops 1086322688 | bytes 18358272 | tf_op jit(solution)/shard_map/while/body/eval_jaxpr/nqkgd,nskd->nkgqs/dot_general | solution.py:64
  61.4 9.2 %fusion.3 = f32[8,256]{1,0:T(8,128)S(1)} fusion(f32[2048,256,8]{1,0,2:T(8,128)} %get-tuple-element.39, f32[8,256]{1,0:T(8,128)S(1)} %get-tuple-element.38, pred[256,2048]{0,1:T(8,128)(4,1)S(1)} %fusion.9), kind=kLoop, calls=%fused_computation.8 | loop fusion | flops 16775168 | bytes 17317888 | tf_op jit(solution)/shard_map/while/body/eval_jaxpr/reduce_sum | solution.py:75
  70.6 8.0 %divide_convert_fusion = bf16[1,256,1,8,128]{1,4,3,2,0:T(8,128)(2,1)S(1)} fusion(f32[2048,256,8]{1,0,2:T(8,128)} %get-tuple-element.39, f32[8,256]{1,0:T(8,128)S(1)} %get-tuple-element.38, pred[256,2048]{0,1:T(8,128)(4,1)S(1)} %fusion.9, bf16[2,2048,128]{2,1,0:T(8,128)(2,1)S(1)} %copy-done.6, f32[256,8]{0,1:T(8,128)S(1)} %bitcast.116), kind=kOutput, calls=%fused_computation.20 | convolution fusion | flops 1091043328 | bytes 18366464 | tf_op jit(solution)/shard_map/while/body/eval_jaxpr/nkgqs,nskd->nqkgd/dot_general | solution.py:76
  80.5 4.5 %all-to-all-start = ((bf16[4,1,256,1024]{3,2,1,0:T(8,128)(2,1)}), bf16[4,1,256,1024]{3,2,1,0:T(8,128)(2,1)S(1)}, u32[]{:S(2)}, u32[]{:S(2)}) async-start(bf16[4,1,256,1024]{3,2,1,0:T(8,128)(2,1)} %broadcast_in_dim.62), calls=%async_computation | async-start | bytes 4194304 | tf_op jit(solution)/shard_map/all_to_all | solution.py:32
  85.0 6.4 %copy.82 = bf16[2048,1024]{1,0:T(8,128)(2,1)} copy(bf16[2048,1024]{0,1:T(8,128)(2,1)} %bitcast.105) | data formatting | bytes 8388608 | tf_op jit(solution)/shard_map/dot_general | solution.py:129
  91.6 20.5 %all-to-all-done = bf16[4,1,256,1024]{3,2,1,0:T(8,128)(2,1)S(1)} async-done(((bf16[4,1,256,1024]{3,2,1,0:T(8,128)(2,1)}), bf16[4,1,256,1024]{3,2,1,0:T(8,128)(2,1)S(1)}, u32[]{:S(2)}, u32[]{:S(2)}) %all-to-all-start) | async-done | bytes 2097184 | tf_op jit(solution)/shard_map/all_to_all | solution.py:32
  114.4 3.0 gather_fusion
  117.5 2.3 fusion.19
  119.8 8.3 %fusion.32 = f32[1024,16,128]{2,0,1:T(8,128)} fusion(bf16[1024,1024,1]{1,0,2:T(8,128)(2,1)S(1)} %bitcast.100, bf16[16,128,1024]{2,1,0:T(8,128)(2,1)} %bitcast.107), kind=kOutput, calls=%fused_computation.47 | convolution fusion | flops 4294967296 | bytes 14680064 | tf_op jit(solution)/shard_map/dot_general | solution.py:129
  128.1 3.4 scatter_fusion
  131.5 11.4 %copy.72 = f32[1024,16,128]{2,1,0:T(8,128)} copy(f32[1024,16,128]{2,0,1:T(8,128)} %scatter_fusion) | data formatting | bytes 16777216 | tf_op jit(solution)/shard_map/scatter-add | solution.py:138
  142.9 9.3 %reshape_reshape.11 = f32[4,256,2048]{2,1,0:T(8,128)} reshape(f32[1024,16,128]{2,1,0:T(8,128)} %copy.72) | data formatting | bytes 16777216 | tf_op jit(solution)/shard_map/reshape;reshape | solution.py:142
  152.2 2.7 fusion.33
  155.0 84.3 %all-reduce.1 = bf16[1024,256]{1,0:T(8,128)(2,1)S(1)} all-reduce(f32[1024,256]{1,0:T(8,128)} %fusion.33), channel_id=1, replica_groups=mesh['row'=4,'col'=8,'seq'=8] {'col'}, use_global_device_ids=true, to_apply=%region_4.5 | all-reduce | flops 262144 | bytes 1572864 | tf_op jit(solution)/shard_map/psum | solution.py:147
  241.0 3.6 %copy.89 = bf16[128,8,16,128]{3,2,1,0:T(8,128)(2,1)S(1)} copy(bf16[128,8,16,128]{3,1,2,0:T(8,128)(2,1)} %bitcast.106) | data formatting | bytes 8388608
  244.7 3.1 copy.73
  247.8 2.8 gather_fusion.1
  252.6 32.5 %all_to_all.16 = f32[8,1,98304]{2,1,0:T(1,128)} all-to-all(f32[8,1,98304]{2,1,0:T(1,128)S(1)} %broadcast_in_dim.63), channel_id=1, replica_groups=mesh['row'=4,'col'=8,'seq'=8] {'seq'}, dimensions={0} | all-to-all | bytes 6291456 | tf_op jit(solution)/shard_map/all_to_all | solution.py:32
  285.1 4.2 %reduce_sum.23 = f32[98304]{0:T(1024)S(1)} reduce(f32[8,1,98304]{2,1,0:T(1,128)} %all_to_all.16, f32[]{:T(128)} %constant.19.clone.1), dimensions={0,1}, to_apply=%region_5.6 | reduce | flops 688128 | bytes 3538948 | tf_op jit(solution)/shard_map/reduce_sum | solution.py:42
  290.9 4.1 %all-to-all-start.2 = ((f32[8,256,256]{2,1,0:T(8,128)}), f32[8,256,256]{2,1,0:T(8,128)S(1)}, u32[]{:S(2)}, u32[]{:S(2)}) async-start(f32[8,256,256]{2,1,0:T(8,128)} %broadcast_in_dim.64), calls=%async_computation.3 | async-start | bytes 4194304 | tf_op jit(solution)/shard_map/all_to_all | solution.py:32
  295.0 2.3 convolution_multiply_fusion
  297.9 38.4 %all-to-all-done.2 = f32[8,256,256]{2,1,0:T(8,128)S(1)} async-done(((f32[8,256,256]{2,1,0:T(8,128)}), f32[8,256,256]{2,1,0:T(8,128)S(1)}, u32[]{:S(2)}, u32[]{:S(2)}) %all-to-all-start.2) | async-done | bytes 2097184 | tf_op jit(solution)/shard_map/all_to_all | solution.py:32
  338.2 3.0 copy.77
  (44 shorter events, 19.8 us)
Async XLA Ops:
  7.2 287.8 %copy-start = (bf16[256,2048]{1,0:T(8,128)(2,1)S(1)}, bf16[256,2048]{1,0:T(8,128)(2,1)}, u32[]{:S(2)}) copy-start(bf16[256,2048]{1,0:T(8,128)(2,1)} %param.16) | copy-start | bytes 3145732
  7.2 46.0 %all-gather.3.cloned.1.call-start = ((), (), s32[]{:S(2)}) async-start(), calls=%async_computation.4 | async-start | bytes 1179648 | tf_op jit(solution)/shard_map/all_gather | solution.py:21
  8.9 232.2 %all-gather.5.cloned.1.call-start = ((), (), s32[]{:S(2)}) async-start(), calls=%async_computation.6 | async-start | bytes 4718592 | tf_op jit(solution)/shard_map/all_gather | solution.py:155
  61.4 9.3 %copy-start.6 = (bf16[2,2048,128]{2,1,0:T(8,128)(2,1)S(1)}, bf16[2,2048,128]{2,1,0:T(8,128)(2,1)}, u32[]{:S(2)}) copy-start(bf16[2,2048,128]{2,1,0:T(8,128)(2,1)} %all-gather.3.cloned.1.call-done) | copy-start | bytes 3145732
  80.5 31.7 %all-to-all-start = ((bf16[4,1,256,1024]{3,2,1,0:T(8,128)(2,1)}), bf16[4,1,256,1024]{3,2,1,0:T(8,128)(2,1)S(1)}, u32[]{:S(2)}, u32[]{:S(2)}) async-start(bf16[4,1,256,1024]{3,2,1,0:T(8,128)(2,1)} %broadcast_in_dim.62), calls=%async_computation | async-start | bytes 4194304 | tf_op jit(solution)/shard_map/all_to_all | solution.py:32
  85.0 256.2 %reduce-scatter.2.cloned.1.call-start = ((), (), s32[]{:S(2)}) async-start(), calls=%async_computation.5 | async-start | bytes 9437184 | tf_op jit(solution)/shard_map/reduce_scatter | solution.py:141
  85.0 6.4 %copy-start.5 = (s32[1,1,2,2]{3,2,1,0:T(2,128)S(1)}, s32[1,1,2,2]{3,2,1,0:T(2,128)}, u32[]{:S(2)}) copy-start(s32[1,1,2,2]{3,2,1,0:T(2,128)} %param.18) | copy-start | bytes 52
  112.2 5.3 %copy-start.4 = (bf16[1,1,2,128,128]{4,3,2,1,0:T(8,128)(2,1)S(1)}, bf16[1,1,2,128,128]{4,3,2,1,0:T(8,128)(2,1)}, u32[]{:S(2)}) copy-start(bf16[1,1,2,128,128]{4,3,2,1,0:T(8,128)(2,1)} %param.17) | copy-start | bytes 196612
  239.3 5.4 %copy-start.3 = (bf16[1024,256]{1,0:T(8,128)(2,1)}, bf16[1024,256]{1,0:T(8,128)(2,1)S(1)}, u32[]{:S(2)}) copy-start(bf16[1024,256]{1,0:T(8,128)(2,1)S(1)} %all-reduce.1) | copy-start | bytes 1572868
  244.7 5.9 %copy-start.1 = (bf16[2,1024,128]{2,1,0:T(8,128)(2,1)S(1)}, bf16[2,1024,128]{2,1,0:T(8,128)(2,1)}, u32[]{:S(2)}) copy-start(bf16[2,1024,128]{2,1,0:T(8,128)(2,1)} %gather_fusion) | copy-start | bytes 1572868
  290.9 45.5 %all-to-all-start.2 = ((f32[8,256,256]{2,1,0:T(8,128)}), f32[8,256,256]{2,1,0:T(8,128)S(1)}, u32[]{:S(2)}, u32[]{:S(2)}) async-start(f32[8,256,256]{2,1,0:T(8,128)} %broadcast_in_dim.64), calls=%async_computation.3 | async-start | bytes 4194304 | tf_op jit(solution)/shard_map/all_to_all | solution.py:32
  338.2 3.0 copy-start.2
Sparse Core Ops, SparseCore 0:
  10.4 42.7 all-gather.2
  54.9 63.4 all-gather.4
  152.4 111.4 reduce-scatter.1
where the time goes:
time: 352 us; the launch traced here: 350 us
  blocking collectives  117 us (33%)
  waiting for transfers between devices  100 us (28%)
  local copies, waits for them, and re-layouts  54.5 us (15%)
  matrix products  33.8 us (10%)
  other arithmetic  22.1 us (6%)
  between operations  14 us (4%)
  starting transfers between devices  8.69 us (2%)
    psum x1, blocking collectives, local(): low_rank_inner = lax.psum(low_rank_piece, 'col').astype(jnp.bfloat16)  84.3 us
    all_to_all x2, waiting for transfers between devices, sent_to_all(): lax.all_to_all(jnp.broadcast_to(shard[None], (peers, *shard.shape)), axis...  58.9 us
    all_gather x1, waiting for transfers between devices, sent_together(): lax.all_gather(both, axis, axis=dim, tiled=True)  40.4 us
    all_to_all x1, blocking collectives, sent_to_all(): lax.all_to_all(jnp.broadcast_to(shard[None], (peers, *shard.shape)), axis...  32.5 us
    scatter-add x1, local copies, waits for them, and re-layouts, local(): partial_value = partial_value.reshape(seq_total, out_tiles, TILE).at[:, t...  11.4 us
    another operation x1, local copies, waits for them, and re-layouts, local(): partial_value.reshape(sequence_rows, local_len, out_width)  9.28 us
    reduce_sum x1, other arithmetic, one_block(): row_total = jnp.sum(weights, axis=-1)  9.25 us
    all_to_all x2, starting transfers between devices, sent_to_all(): lax.all_to_all(jnp.broadcast_to(shard[None], (peers, *shard.shape)), axis...  8.61 us
  transfers between devices with their start and end apart: 5, of which 3 were waited for; matrix products, arithmetic and copies ran while one was open for 30% of the time, Pallas kernels for 0%

commit v1 on v0

v1 whole, which is shorter than its diff:
```python
import functools

import jax
import jax.numpy as jnp
from jax import lax
from jax.experimental import pallas as pl
from jax.experimental.pallas import tpu as pltpu
from jax.sharding import PartitionSpec as P

HEAD_WIDTH = 128
TILE = 128
MESH = pl.DeviceIdType.MESH
BF = jnp.bfloat16
F32 = jnp.float32
LOW_RANK_FACTOR = 2.0
EXP_SCALE = HEAD_WIDTH ** -0.5 * 1.4426950408889634
HIDDEN = -1e30


def dot(a, b, dims=((1,), (0,))):
    return lax.dot_general(a, b, (dims, ((), ())), preferred_element_type=F32)


def kernel(
    place, doc, q, k_hbm, v_hbm, w_hbm, d_hbm, u_hbm, t_hbm, cot_hbm,
    out, up_out, gt_out,
    kwin, vwin, bias, attn, cotall, w, d, u, tiles, cblk, snd, rcv, choice, picked, picked_t, lr_part, lr_recv, lr_full,
    sum_src, sum_recv, up_full, gt_full,
    kv_s, kv_r, loc, cot_s, cot_r, row_s, row_r, rs_s, rs_r, lr_s, lr_r, lb_s, lb_r, lw_s, lw_r,
    ss_s, ss_r, uz_s, uz_r, us_s, us_r, gs_s, gs_r,
):
    r, c, s = lax.axis_index("row"), lax.axis_index("col"), lax.axis_index("seq")

    def remote(src, dst, send, recv, row=None, col=None, seq=None):
        return pltpu.make_async_remote_copy(
            src_ref=src,
            dst_ref=dst,
            send_sem=send,
            recv_sem=recv,
            device_id=(r if row is None else row, c if col is None else col, s if seq is None else seq),
            device_id_type=MESH,
        )

    def mul(x, n):
        return pl.multiple_of(x * n, n)

    barrier = pltpu.get_barrier_semaphore()
    for o in range(1, 8):
        pl.semaphore_signal(barrier, inc=1, device_id=(r, c, (s + o) % 8), device_id_type=MESH)
        pl.semaphore_signal(barrier, inc=1, device_id=(r, (c + o) % 8, s), device_id_type=MESH)
    for o in range(1, 4):
        pl.semaphore_signal(barrier, inc=1, device_id=((r + o) % 4, c, s), device_id_type=MESH)
    pl.semaphore_wait(barrier, 17)

    kv = []
    for j in (1, 2, 3, 4):
        at = pl.ds((4 - j) * 256, 256)
        kv.append(remote(k_hbm, kwin.at[at], kv_s.at[j - 1, 0], kv_r.at[j - 1, 0], seq=(s + j) % 8))
        kv.append(remote(v_hbm, vwin.at[at], kv_s.at[j - 1, 1], kv_r.at[j - 1, 1], seq=(s + j) % 8))
        kv[-2].start()
        kv[-1].start()

    cot_order = [[(1, 0), (1, 1), (2, 0), (2, 1), (3, 0), (3, 1), (4, 0)],
                 [(1, 1), (1, 0), (2, 1), (2, 0), (3, 1), (3, 0), (4, 1)]]
    signs = (1, -1)

    def cot_copy(way, m):
        step, half = cot_order[way][m]
        owner = (c - signs[way] * (step - 1) + 8) % 8
        rows = pl.ds(half * 512, 512)
        src = cot_hbm.at[rows] if step == 1 else cotall.at[owner, rows]
        return remote(src, cotall.at[owner, rows], cot_s.at[way, m], cot_r.at[way, m],
                      col=(c + signs[way] + 8) % 8)

    cot = [[cot_copy(way, m) for m in range(7)] for way in range(2)]
    for m in range(2):
        for way in range(2):
            cot[way][m].start()

    def cot_forward(m):
        for way in range(2):
            cot[way][m].wait_recv()
            cot[way][m + 2].start()

    locals_ = [
        pltpu.make_async_copy(src, dst, loc.at[i])
        for i, (src, dst) in enumerate(
            (
                (k_hbm, kwin.at[pl.ds(1024, 256)]),
                (v_hbm, vwin.at[pl.ds(1024, 256)]),
                (d_hbm, d),
                (cot_hbm, cotall.at[c]),
                (t_hbm, tiles),
                (u_hbm.at[:, pl.ds(mul(c, 256), 256)], u),
                (w_hbm, w),
            )
        )
    ]
    for copy in locals_:
        copy.start()

    own_doc = doc[:, pl.ds(mul(s, 256), 256)].astype(F32)
    column = jnp.broadcast_to(own_doc, (128, 256)).T[:, :1]
    for slot in range(5):
        block = s - 4 + slot
        key_doc = doc[:, pl.ds(mul((block + 8) % 8, 256), 256)].astype(F32)
        key_at = block * 256 + lax.broadcasted_iota(jnp.int32, (256, 256), 1)
        query_at = s * 256 + lax.broadcasted_iota(jnp.int32, (256, 256), 0)
        seen = (key_at >= 0) & (key_at <= query_at) & (column == key_doc)
        bias[:, slot * 256 : slot * 256 + 256] = jnp.where(seen, 0.0, HIDDEN)

    for t in range(2):
        row = lax.broadcasted_iota(jnp.int32, (128, 1024), 0)
        lane = lax.broadcasted_iota(jnp.int32, (128, 1024), 1)
        wanted = jnp.full((128, 1024), place[t, 0], jnp.int32) * 128 + row
        choice[t * 128 : t * 128 + 128, :] = jnp.where(lane == wanted, 1.0, 0.0).astype(BF)

    locals_[0].wait()
    locals_[1].wait()
    for copy in kv[:4]:
        copy.wait_recv()
    cot_forward(0)
    for copy in kv[4:]:
        copy.wait_recv()

    own_rows = pl.ds(mul(r, 256), 256)

    def head(h, carry):
        at = pl.ds(mul(h, 128), 128)
        scores = dot(q[:, at], kwin[...], ((1,), (1,))) + bias[...]
        top = jnp.max(scores, axis=1, keepdims=True)
        probs = jnp.exp2((scores - top) * EXP_SCALE)
        total = jnp.sum(probs, axis=1, keepdims=True)
        mixed = dot(probs.astype(BF), vwin[...])
        attn[own_rows, at] = (mixed / total).astype(BF)
        return carry

    sibling, opposite = r + 1 - 2 * (r % 2), (r + 2) % 4
    shared, crossed, relayed = [], [], []
    for p in range(4):
        lanes = pl.ds(p * 256, 256)
        mine = attn.at[own_rows, lanes]
        other = attn.at[pl.ds(mul(opposite, 256), 256), lanes]
        shared.append(remote(mine, mine, row_s.at[0, p], row_r.at[0, p], row=sibling))
        crossed.append(remote(mine, mine, row_s.at[1, p], row_r.at[1, p], row=opposite))
        relayed.append(remote(other, other, row_s.at[2, p], row_r.at[2, p], row=sibling))

    def relay(p):
        crossed[p].wait_recv()
        relayed[p].start()

    for p in range(4):
        lax.fori_loop(2 * p, 2 * p + 2, head, 0)
        crossed[p].start()
        shared[p].start()
        if p == 0:
            cot_forward(1)
        if p == 2:
            cot_forward(2)

    locals_[2].wait()
    lr_part[...] = dot(attn[own_rows, :], d[...]).astype(BF).reshape(8, 32, 256)
    lr = [
        remote(lr_part.at[(c + o) % 8], lr_recv.at[o - 1], lr_s.at[o - 1], lr_r.at[o - 1], col=(c + o) % 8)
        for o in range(1, 8)
    ]
    for copy in lr:
        copy.start()
    relay(0)
    relay(1)
    for copy in lr:
        copy.wait_recv()
    piece_at = pl.ds(mul(c, 32), 32)
    lr_full[r, piece_at, :] = (lr_part[c].astype(F32) + jnp.sum(lr_recv[...].astype(F32), axis=0)).astype(BF)
    piece = lr_full.at[r, piece_at]
    lb = [remote(piece, piece, lb_s.at[o - 1], lb_r.at[o - 1], col=(c + o) % 8) for o in range(1, 8)]
    for copy in lb:
        copy.start()
    cot_forward(3)
    relay(2)
    relay(3)
    for copy in lb:
        copy.wait_recv()
    lw = [remote(lr_full.at[r], lr_full.at[r], lw_s.at[o - 1], lw_r.at[o - 1], row=(r + o) % 4) for o in range(1, 4)]
    for copy in lw:
        copy.start()
    cot_forward(4)

    for copy in shared + relayed:
        copy.wait_recv()
    for copy in locals_[3:]:
        copy.wait()

    def pick(h, carry):
        rows = pl.ds(mul(h, 512), 512)
        picked[rows, :] = dot(attn[rows, :], choice[...], ((1,), (1,))).astype(BF)
        picked_t[:, rows] = dot(choice[...], attn[rows, :], ((1,), (1,))).astype(BF)
        return carry

    lax.fori_loop(0, 2, pick, 0)

    def partial(o):
        block = (c + o) % 8
        grid = []
        for t in range(2):
            at = jnp.full((128, 128), place[t, 1], jnp.int32)
            tile = tiles[t].astype(F32)
            grid.append(
                jnp.concatenate([jnp.where(at == 2 * block + i, tile, 0.0) for i in range(2)], axis=1)
            )
        placed = jnp.concatenate(grid, axis=0).astype(BF)
        lanes = pl.ds(mul(block, 256), 256)

        def half(h, carry):
            rows = pl.ds(mul(h, 512), 512)
            cblk[o, rows, :] = dot(attn[rows, :], w[:, lanes]) + dot(picked[rows, :], placed)
            return carry

        lax.fori_loop(0, 2, half, 0)

    def rs_order(way):
        p, n = (0, 1) if way == 0 else (1, 0)
        return [(1, p), (2, n), (2, p), (3, n), (3, p), (4, n), (4, p)]

    rs = [
        [
            remote(snd.at[way, m], rcv.at[way, m], rs_s.at[way, m], rs_r.at[way, m], col=(c + signs[way] + 8) % 8)
            for m in range(7)
        ]
        for way in range(2)
    ]

    def rs_send(m):
        for way in range(2):
            step, half = rs_order(way)[m]
            o = (signs[way] * (5 - step)) % 8
            if m >= 2:
                rs[way][m - 2].wait_recv()

            def chunk(i, carry):
                rows = pl.ds(mul(i, 128), 128)
                value = cblk[o, pl.ds(half * 512 + mul(i, 128), 128), :]
                if m >= 2:
                    value = value + rcv[way, m - 2, rows, :].astype(F32)
                snd[way, m, rows, :] = value.astype(BF)
                return carry

            lax.fori_loop(0, 4, chunk, 0)
            rs[way][m].start()

    partial(4)
    rs_send(0)
    partial(3)
    partial(5)
    rs_send(1)

    for copy in lw:
        copy.wait_recv()
    up_piece = LOW_RANK_FACTOR * dot(lr_full[...].reshape(1024, 256), cotall[c], ((0,), (0,)))
    sum_src[:, :, :256] = up_piece.reshape(8, 32, 256)
    partial(2)
    partial(6)
    for m in (5, 6):
        for way in range(2):
            cot[way][m].wait_recv()
    rs_send(2)

    def tile_grads(owner, carry):
        grads = dot(picked_t[...], cotall[owner])
        kept = []
        for t in range(2):
            value = carry[t]
            for i in range(2):
                at = jnp.full((128, 128), place[t, 1], jnp.int32)
                part = grads[t * 128 : t * 128 + 128, i * 128 : i * 128 + 128]
                value = jnp.where(at == 2 * owner + i, part, value)
            kept.append(value)
        return tuple(kept)

    grads = lax.fori_loop(0, 8, tile_grads, (jnp.zeros((128, 128), F32),) * 2)
    for t in range(2):
        sum_src[t * 4 : t * 4 + 4, :, 256:] = grads[t].reshape(4, 32, 128)
    ss = [
        remote(sum_src.at[(s + o) % 8], sum_recv.at[o - 1], ss_s.at[o - 1], ss_r.at[o - 1], seq=(s + o) % 8)
        for o in range(1, 8)
    ]
    for copy in ss:
        copy.start()
    rs_send(3)
    partial(1)
    partial(7)
    for copy in ss:
        copy.wait_recv()
    total = sum_src[s] + jnp.sum(sum_recv[...], axis=0)
    seq_rows = pl.ds(mul(s, 32), 32)
    col_lanes = pl.ds(mul(c, 256), 256)
    up_full[seq_rows, col_lanes] = total[:, :256].astype(BF)
    gt_full[seq_rows, :] = total[:, 256:]
    up_at, gt_at = up_full.at[seq_rows, col_lanes], gt_full.at[seq_rows]
    uz = [remote(up_at, up_at, uz_s.at[o - 1], uz_r.at[o - 1], col=(c + o) % 8) for o in range(1, 8)]
    gs = [remote(gt_at, gt_at, gs_s.at[o - 1], gs_r.at[o - 1], seq=(s + o) % 8) for o in range(1, 8)]
    for copy in uz + gs:
        copy.start()
    rs_send(4)
    partial(0)

    def low_rank_half(h, carry):
        rows = pl.ds(mul(h, 512), 512)
        inner = lr_full[pl.ds(2 * h, 2)].reshape(512, 256)
        cblk[0, rows, :] = cblk[0, rows, :] + LOW_RANK_FACTOR * dot(inner, u[...])
        return carry

    lax.fori_loop(0, 2, low_rank_half, 0)
    for copy in uz:
        copy.wait_recv()
    seq_at = up_full.at[seq_rows]
    us = [remote(seq_at, seq_at, us_s.at[o - 1], us_r.at[o - 1], seq=(s + o) % 8) for o in range(1, 8)]
    for copy in us:
        copy.start()
    rs_send(5)
    rs_send(6)
    for copy in us + gs:
        copy.wait_recv()
    gt_out[...] = gt_full[...]
    up_copy = pltpu.make_async_copy(up_full, up_out, loc.at[0])
    up_copy.start()
    for m in (5, 6):
        for way in range(2):
            rs[way][m].wait_recv()

    def finish(i, carry):
        for half in range(2):
            rows = pl.ds(mul(i, 128), 128)
            at = pl.ds(half * 512 + mul(i, 128), 128)
            there = [rcv[way, 6 if half == way else 5, rows, :].astype(F32) for way in range(2)]
            out[at, :] = (cblk[0, at, :] + (there[0] + there[1])).astype(BF)
        return carry

    lax.fori_loop(0, 4, finish, 0)
    up_copy.wait()
    for copy in kv + cot[0] + cot[1] + shared + crossed + relayed + lr + lb + lw + rs[0] + rs[1] + ss + uz + gs + us:
        copy.wait_send()


def hand_over(out, up_grad, tile_grad, out_to, up_to, tile_to):
    out_to[...] = out[...]
    up_to[...] = up_grad[...].astype(F32)
    tile_to[...] = tile_grad[...]


def local(queries, keys, values, documents, weight, down, up, tiles, placement, cotangent):
    dma = pltpu.SemaphoreType.DMA
    vmem = pltpu.VMEM
    anywhere = pl.BlockSpec(memory_space=pl.ANY)
    in_vmem = pl.BlockSpec(memory_space=pltpu.VMEM)
    out, up_grad, tile_grad = pl.pallas_call(
        kernel,
        out_shape=(
            jax.ShapeDtypeStruct((1024, 256), BF),
            jax.ShapeDtypeStruct((256, 2048), BF),
            jax.ShapeDtypeStruct((256, 128), F32),
        ),
        in_specs=[pl.BlockSpec(memory_space=pltpu.SMEM), in_vmem, in_vmem] + [anywhere] * 7,
        out_specs=(in_vmem, anywhere, in_vmem),
        scratch_shapes=[
            vmem((1280, 128), BF), vmem((1280, 128), BF), vmem((256, 1280), F32), vmem((1024, 1024), BF),
            vmem((8, 1024, 256), BF), vmem((1024, 2048), BF), vmem((1024, 256), BF), vmem((256, 256), BF),
            vmem((2, 128, 128), BF), vmem((8, 1024, 256), F32), vmem((2, 7, 512, 256), BF),
            vmem((2, 7, 512, 256), BF), vmem((256, 1024), BF), vmem((1024, 256), BF), vmem((256, 1024), BF), vmem((8, 32, 256), BF), vmem((7, 32, 256), BF),
            vmem((4, 256, 256), BF), vmem((8, 32, 384), F32), vmem((7, 32, 384), F32), vmem((256, 2048), BF),
            vmem((256, 128), F32),
            dma((4, 2)), dma((4, 2)), dma((7,)), dma((2, 7)), dma((2, 7)), dma((3, 4)), dma((3, 4)),
            dma((2, 7)), dma((2, 7)), dma((7,)), dma((7,)), dma((7,)), dma((7,)), dma((3,)), dma((3,)),
            dma((7,)), dma((7,)), dma((7,)), dma((7,)), dma((7,)), dma((7,)), dma((7,)), dma((7,)),
        ],
        compiler_params=pltpu.CompilerParams(
            collective_id=0, has_side_effects=True, vmem_limit_bytes=60 * 1024 * 1024
        ),
    )(
        placement.reshape(2, 2),
        documents,
        queries.reshape(256, 1024),
        keys.reshape(256, 128),
        values.reshape(256, 128),
        weight,
        down,
        up,
        tiles.reshape(2, 128, 128),
        cotangent.reshape(1024, 256),
    )
    steps = 4
    results = ((1024, 256, BF), (256, 2048, F32), (256, 128, F32))
    specs = [pl.BlockSpec((rows // steps, lanes), lambda i: (i, 0)) for rows, lanes, _ in results]
    out, up_grad, tile_grad = pl.pallas_call(
        hand_over,
        grid=(steps,),
        out_shape=tuple(jax.ShapeDtypeStruct((rows, lanes), kind) for rows, lanes, kind in results),
        in_specs=specs,
        out_specs=tuple(specs),
    )(out, up_grad, tile_grad)
    return (
        out.reshape(4, 256, 256),
        up_grad,
        tile_grad.reshape(1, 1, 2, 128, 128),
    )


def solution(mesh):
    placed = (
        P("row", "seq", "col"),
        P("row", "seq", "col"),
        P("row", "seq", "col"),
        P("row", None),
        P("col", "row"),
        P("col", None),
        P(None, "row"),
        P("row", "col", None, None, None),
        P("row", "col", None, None),
        P(None, "seq", ("row", "col")),
    )
    return jax.shard_map(
        local,
        mesh=mesh,
        in_specs=placed,
        out_specs=(
            P(None, "seq", ("row", "col")),
            P(None, "row"),
            P("row", "col", None, None, None),
        ),
        check_vma=False,
    )
```

time: 352 us -> 107 us (0.30)
  blocking collectives: 117 us -> 0 us
  Pallas kernels: 0 us -> 107 us
  waiting for transfers between devices: 100 us -> 0 us
  local copies, waits for them, and re-layouts: 54.5 us -> 0 us
  matrix products: 33.8 us -> 0 us
  other arithmetic: 22.1 us -> 0 us
  between operations: 14 us -> 0.64 us
  starting transfers between devices: 8.69 us -> 0 us
    pallas_call x0 -> x2, Pallas kernels: none -> 107 us  [the longest x1 103 us: local(): pl.pallas_call(kernel, out_shape=(jax.ShapeDtypeStruct((1024, 256), BF),...]
    psum x1 -> x0, blocking collectives: 84.3 us -> none  [local(): low_rank_inner = lax.psum(low_rank_piece, 'col').astype(jnp.bfloat16)]
    all_to_all x2 -> x0, waiting for transfers between devices: 58.9 us -> none  [sent_to_all(): lax.all_to_all(jnp.broadcast_to(shard[None], (peers, *shard.shape)), axis...]
    all_gather x2 -> x0, waiting for transfers between devices: 40.4 us -> none  [the longest x1 40.4 us: sent_together(): lax.all_gather(both, axis, axis=dim, tiled=True)]
    dot_general x8 -> x0, matrix products: 33.8 us -> none  [the longest x1 8.32 us: local(): jnp.dot(flattened_rows, output_projection_weight, preferred_element_type=...]
    all_to_all x1 -> x0, blocking collectives: 32.5 us -> none  [sent_to_all(): lax.all_to_all(jnp.broadcast_to(shard[None], (peers, *shard.shape)), axis...]
    another operation x3 -> x0, local copies, waits for them, and re-layouts: 14 us -> none  [the longest x1 9.28 us: local(): partial_value.reshape(sequence_rows, local_len, out_width)]
    reduce_sum x2 -> x0, other arithmetic: 13.4 us -> none  [the longest x1 9.25 us: one_block(): row_total = jnp.sum(weights, axis=-1)]
  transfers between devices with their start and end apart: 5 -> 0, of which waited for: 3 -> 0; matrix products, arithmetic and copies ran while one was open for 30% -> 0% of each run, Pallas kernels for 0% -> 0%
where the time goes in v1:
time: 107 us
  Pallas kernels  107 us (100%)
    pallas_call x1, Pallas kernels, local(): pl.pallas_call(kernel, out_shape=(jax.ShapeDtypeStruct((1024, 256), BF),...  103 us
    pallas_call x1, Pallas kernels, local(): pl.pallas_call(hand_over, grid=(steps,), out_shape=tuple((jax.ShapeDtypeS...  3.77 us

profile of v1, /device:TPU:6, one launch (start us, length us, event | category | flops | bytes accessed | tf_op | source)
XLA Modules:
  0.0 107.2 jit_solution(15602135863568124403)
XLA Ops:
  0.6 102.8 %shard_map.121 = (bf16[1024,256]{1,0:T(8,128)(2,1)}, bf16[256,2048]{1,0:T(8,128)(2,1)}, f32[256,128]{1,0:T(8,128)}) custom-call(s32[2,2]{1,0:T(2,128)} %bitcast.13, s32[1,2048]{1,0:T(1,128)} %doc.1, bf16[256,1024]{1,0:T(8,128)(2,1)} %bitcast.8, bf16[256,128]{1,0:T(8,128)(2,1)} %bitcast.10, bf16[256,128]{1,0:T(8,128)(2,1)} %bitcast.11, ...), custom_call_target="tpu_custom_call" | custom-call | tf_op jit(solution)/shard_map/pallas_call | solution.py:356
  103.4 3.8 %shard_map.122 = (bf16[1024,256]{1,0:T(8,128)(2,1)}, f32[256,2048]{1,0:T(8,128)}, f32[256,128]{1,0:T(8,128)}) custom-call(bf16[1024,256]{1,0:T(8,128)(2,1)} %get-tuple-element.9.out, bf16[256,2048]{1,0:T(8,128)(2,1)} %get-tuple-element.10.up_grad, f32[256,128]{1,0:T(8,128)} %get-tuple-element.11.tile_grad), custom_call_target="tpu_custom_call" | custom-call | tf_op jit(solution)/shard_map/pallas_call | solution.py:394

commit v2 on v1

--- a/solution.py
+++ b/solution.py
@@ -24,7 +24,7 @@
 def kernel(
     place, doc, q, k_hbm, v_hbm, w_hbm, d_hbm, u_hbm, t_hbm, cot_hbm,
     out, up_out, gt_out,
-    kwin, vwin, bias, attn, cotall, w, d, u, tiles, cblk, snd, rcv, choice, picked, picked_t, lr_part, lr_recv, lr_full,
+    kwin, vwin, vt, bias, attn, cotall, w, d, u, tiles, cblk, snd, rcv, choice, picked, picked_t, lr_part, lr_recv, lr_full,
     sum_src, sum_recv, up_full, gt_full,
     kv_s, kv_r, loc, cot_s, cot_r, row_s, row_r, rs_s, rs_r, lr_s, lr_r, lb_s, lb_r, lw_s, lw_r,
     ss_s, ss_r, uz_s, uz_r, us_s, us_r, gs_s, gs_r,
@@ -100,14 +100,15 @@
         copy.start()
 
     own_doc = doc[:, pl.ds(mul(s, 256), 256)].astype(F32)
-    column = jnp.broadcast_to(own_doc, (128, 256)).T[:, :1]
     for slot in range(5):
         block = s - 4 + slot
         key_doc = doc[:, pl.ds(mul((block + 8) % 8, 256), 256)].astype(F32)
-        key_at = block * 256 + lax.broadcasted_iota(jnp.int32, (256, 256), 1)
-        query_at = s * 256 + lax.broadcasted_iota(jnp.int32, (256, 256), 0)
-        seen = (key_at >= 0) & (key_at <= query_at) & (column == key_doc)
-        bias[:, slot * 256 : slot * 256 + 256] = jnp.where(seen, 0.0, HIDDEN)
+        column = jnp.broadcast_to(key_doc, (128, 256)).T
+        column = jnp.concatenate([column, column], axis=1)
+        key_at = block * 256 + lax.broadcasted_iota(jnp.int32, (256, 256), 0)
+        query_at = s * 256 + lax.broadcasted_iota(jnp.int32, (256, 256), 1)
+        seen = (key_at >= 0) & (key_at <= query_at) & (column == own_doc)
+        bias[slot * 256 : slot * 256 + 256, :] = jnp.where(seen, 0.0, HIDDEN)
 
     for t in range(2):
         row = lax.broadcasted_iota(jnp.int32, (128, 1024), 0)
@@ -123,17 +124,17 @@
     for copy in kv[4:]:
         copy.wait_recv()
 
+    vt[...] = vwin[...].astype(F32).T.astype(BF)
     own_rows = pl.ds(mul(r, 256), 256)
 
-    def head(h, carry):
-        at = pl.ds(mul(h, 128), 128)
-        scores = dot(q[:, at], kwin[...], ((1,), (1,))) + bias[...]
-        top = jnp.max(scores, axis=1, keepdims=True)
+    def head(h):
+        at = slice(h * 128, h * 128 + 128)
+        scores = dot(kwin[...], q[:, at], ((1,), (1,))) + bias[...]
+        top = jnp.max(scores, axis=0, keepdims=True)
         probs = jnp.exp2((scores - top) * EXP_SCALE)
-        total = jnp.sum(probs, axis=1, keepdims=True)
-        mixed = dot(probs.astype(BF), vwin[...])
-        attn[own_rows, at] = (mixed / total).astype(BF)
-        return carry
+        total = jnp.sum(probs, axis=0, keepdims=True)
+        mixed = dot(vt[...], probs.astype(BF)) / total
+        attn[own_rows, at] = mixed.T.astype(BF)
 
     sibling, opposite = r + 1 - 2 * (r % 2), (r + 2) % 4
     shared, crossed, relayed = [], [], []
@@ -150,7 +151,8 @@
         relayed[p].start()
 
     for p in range(4):
-        lax.fori_loop(2 * p, 2 * p + 2, head, 0)
+        head(2 * p)
+        head(2 * p + 1)
         crossed[p].start()
         shared[p].start()
         if p == 0:
@@ -363,7 +365,7 @@
         in_specs=[pl.BlockSpec(memory_space=pltpu.SMEM), in_vmem, in_vmem] + [anywhere] * 7,
         out_specs=(in_vmem, anywhere, in_vmem),
         scratch_shapes=[
-            vmem((1280, 128), BF), vmem((1280, 128), BF), vmem((256, 1280), F32), vmem((1024, 1024), BF),
+            vmem((1280, 128), BF), vmem((1280, 128), BF), vmem((128, 1280), BF), vmem((1280, 256), F32), vmem((1024, 1024), BF),
             vmem((8, 1024, 256), BF), vmem((1024, 2048), BF), vmem((1024, 256), BF), vmem((256, 256), BF),
             vmem((2, 128, 128), BF), vmem((8, 1024, 256), F32), vmem((2, 7, 512, 256), BF),
             vmem((2, 7, 512, 256), BF), vmem((256, 1024), BF), vmem((1024, 256), BF), vmem((256, 1024), BF), vmem((8, 32, 256), BF), vmem((7, 32, 256), BF),
@@ -388,7 +390,7 @@
         tiles.reshape(2, 128, 128),
         cotangent.reshape(1024, 256),
     )
-    steps = 4
+    steps = 2
     results = ((1024, 256, BF), (256, 2048, F32), (256, 128, F32))
     specs = [pl.BlockSpec((rows // steps, lanes), lambda i: (i, 0)) for rows, lanes, _ in results]
     out, up_grad, tile_grad = pl.pallas_call(

time: 107 us -> 106 us (level)
  Pallas kernels: 107 us -> 105 us
where the time goes in v2:
time: 106 us
  Pallas kernels  105 us (99%)
    pallas_call x1, Pallas kernels, local(): pl.pallas_call(kernel, out_shape=(jax.ShapeDtypeStruct((1024, 256), BF),...  103 us
    pallas_call x1, Pallas kernels, local(): pl.pallas_call(hand_over, grid=(steps,), out_shape=tuple((jax.ShapeDtypeS...  2.73 us

profile of v2, /device:TPU:6, one launch (start us, length us, event | category | flops | bytes accessed | tf_op | source)
XLA Modules:
  0.0 106.1 jit_solution(10588327584454540757)
XLA Ops:
  0.6 102.8 %shard_map.121 = (bf16[1024,256]{1,0:T(8,128)(2,1)}, bf16[256,2048]{1,0:T(8,128)(2,1)}, f32[256,128]{1,0:T(8,128)}) custom-call(s32[2,2]{1,0:T(2,128)} %bitcast.13, s32[1,2048]{1,0:T(1,128)} %doc.1, bf16[256,1024]{1,0:T(8,128)(2,1)} %bitcast.8, bf16[256,128]{1,0:T(8,128)(2,1)} %bitcast.10, bf16[256,128]{1,0:T(8,128)(2,1)} %bitcast.11, ...), custom_call_target="tpu_custom_call" | custom-call | tf_op jit(solution)/shard_map/pallas_call | solution.py:358
  103.4 2.7 %shard_map.122 = (bf16[1024,256]{1,0:T(8,128)(2,1)}, f32[256,2048]{1,0:T(8,128)}, f32[256,128]{1,0:T(8,128)}) custom-call(bf16[1024,256]{1,0:T(8,128)(2,1)} %get-tuple-element.9.out, bf16[256,2048]{1,0:T(8,128)(2,1)} %get-tuple-element.10.up_grad, f32[256,128]{1,0:T(8,128)} %get-tuple-element.11.tile_grad), custom_call_target="tpu_custom_call" | custom-call | tf_op jit(solution)/shard_map/pallas_call | solution.py:396
